TPU v7x, 256 devices: a whole 4x4x8 slice. The times are simulated.
256 devices in a mesh: dp: 16 (over z, core), frame: 16 (over y, x).
Axes of the slice: x: 4, y: 4, z: 8, core: 2. Of those that a mesh axis runs over, the one named last changes fastest.
Arguments:
- latents: bfloat16 [16, 16, 512, 640], P('dp', 'frame'), may hold values from -6 to 6
- cotangent: bfloat16 [16, 16, 512, 640], P('dp', 'frame'), may hold values from -6 to 6
- timesteps: int32 [16], P('dp'), may hold values from 0 to 999
- spatial_weight: bfloat16 [9, 640, 640], replicated, may hold values from -0.078125 to 0.078125
- temporal_weight: bfloat16 [3, 640, 640], replicated, may hold values from -0.125 to 0.125
Outputs:
- new_spatial: float32 [9, 640, 640], P(None, 'frame')
- new_temporal: float32 [3, 640, 640], P(None, 'frame')
All inputs are finite; a program needn't handle non-finite values.
Results may differ from a plain program's by a relative error of at most 0.02.
Values may be sent and summed in bfloat16 or wider, within the bound.
No kernel may reach another device: no remote copies, remote signals or barrier semaphores. Data moves between devices by JAX's collectives and lax.ppermute only.
A program may use at most 128 MiB of HBM per device.

v0:
```python
import math

import jax
import jax.numpy as jnp
from jax import lax
from jax.experimental import pallas as pl
from jax.experimental.pallas import tpu as pltpu
from jax.sharding import Mesh
from jax.sharding import PartitionSpec as P


WIDTH = 64
F32 = jnp.float32
BF16 = jnp.bfloat16
SIZES = {"z": 8, "core": 2, "y": 4, "x": 4}


def embed(timesteps, channels):
    half_width = channels // 2
    frequencies = jnp.exp(
        -math.log(10000.0) * jnp.arange(half_width, dtype=jnp.float32) / half_width
    )
    angles = timesteps.astype(jnp.float32)[:, None] * frequencies[None, :]
    return jnp.concatenate([jnp.sin(angles), jnp.cos(angles)], axis=1)


def clip_factor(squares, channels):
    max_norm = 0.5 * math.sqrt(12.0) * channels
    return jnp.minimum(1.0, max_norm / (jnp.sqrt(squares) + 1e-06))


def hop(value, axis, step):
    size = SIZES[axis]
    return lax.ppermute(value, axis, [(i, (i + step) % size) for i in range(size)])


def add(left, right):
    return (left.astype(F32) + right.astype(F32)).astype(BF16)


def both_ways(up, down, axis):
    up = hop(up, axis, 1)
    down = hop(down, axis, 3)
    return up, down


def ring_open(share, axis):
    far = share(2)
    half = far.shape[0] // 2
    return both_ways(far[:half], far[half:], axis)


def ring_close(share, axis, from_left, from_right):
    half = from_left.shape[0]
    ahead = share(1)
    behind = share(3)
    ahead = jnp.concatenate([add(ahead[:half], from_left), ahead[half:]], 0)
    behind = jnp.concatenate([behind[:half], add(behind[half:], from_right)], 0)
    from_left, from_right = both_ways(ahead, behind, axis)
    return (share(0).astype(F32) + from_left.astype(F32) + from_right.astype(F32)).astype(BF16)


def direct_scatter(share, axis):
    far = hop(share(2), axis, 2)
    left = hop(share(1), axis, 1)
    right = hop(share(3), axis, 3)
    total = share(0).astype(F32) + left.astype(F32) + right.astype(F32) + far.astype(F32)
    return total.astype(BF16)


def shift_rows(value, by):
    rows = value.shape[1]
    if by == 0:
        return value
    if by > 0:
        return jnp.pad(value[:, by:], ((0, 0), (0, by), (0, 0)))
    return jnp.pad(value[:, : rows + by], ((0, 0), (-by, 0), (0, 0)))


def shift_cols(value, by):
    if by == 0:
        return value
    q = lax.broadcasted_iota(jnp.int32, (1, value.shape[1], 1), 1) % WIDTH
    edge = q == (WIDTH - 1 if by > 0 else 0)
    return jnp.where(edge, jnp.zeros((), value.dtype), shift_rows(value, by))


def rows_dot(left, right):
    return lax.dot_general(left, right, (((0,), (0,)), ((), ())), preferred_element_type=F32)


def store_shares(axis, place, step, acc, shares):
    block = acc.shape[0] // 16
    for j, share in enumerate(shares):
        owner = lax.rem(place + j, 4)
        for k in range(4):
            start = (k * 4 + owner) * block if axis == "x" else (owner * 4 + k) * block
            rows = acc[pl.ds(pl.multiple_of(start, 8), block), :]
            share[k, step] = rows.astype(BF16)


def edge_kernel(where, turned, turned_far, grad, grad_far, *refs):
    *shares, acc = refs
    step = pl.program_id(0)
    inner = grad.shape[0] - WIDTH
    top = pl.multiple_of((1 + where[0]) * WIDTH, WIDTH)
    below = pl.multiple_of((1 - where[0]) * WIDTH, WIDTH)
    acc[...] = rows_dot(turned[0, pl.ds(top, inner), :], grad[pl.ds(below, inner), :])
    acc[...] += rows_dot(turned_far[0, pl.ds(top, inner), :], grad_far[pl.ds(below, inner), :])
    store_shares("x", where[1], step, acc, shares)


def mixed_kernel(where, turned, turned_far, grad, grad_far, cots, gate, cots_far, gate_far, *refs):
    *shares, acc = refs
    step = pl.program_id(0)
    pixels = grad.shape[0]

    @pl.when(where[0] == 0)
    def _():
        acc[...] = rows_dot(turned[0, WIDTH : WIDTH + pixels, :], grad[...])
        acc[...] += rows_dot(turned_far[0, WIDTH : WIDTH + pixels, :], grad_far[...])

    @pl.when(where[0] == 1)
    def _():
        acc[...] = rows_dot(gate[0], cots[0])
        acc[...] += rows_dot(gate_far[0], cots_far[0])

    store_shares("y", where[1], step, acc, shares)


def taps(kernel, where, arrays, blocks):
    channels = arrays[0].shape[-1]
    block = channels // 16

    def spec(array, lead):
        if lead is None:
            return pl.BlockSpec(array.shape, lambda e, where: (0,) * array.ndim)
        return pl.BlockSpec((1,) + array.shape[1:], lambda e, where: (lead(e), 0, 0))

    share = jax.ShapeDtypeStruct((4, 3, block, channels), BF16)
    out = pl.pallas_call(
        kernel,
        out_shape=[share] * 4,
        grid_spec=pltpu.PrefetchScalarGridSpec(
            num_scalar_prefetch=1,
            grid=(3,),
            in_specs=[spec(a, b) for a, b in zip(arrays, blocks)],
            out_specs=[pl.BlockSpec(share.shape, lambda e, where: (0, 0, 0, 0))] * 4,
            scratch_shapes=[pltpu.VMEM((channels, channels), F32)],
        ),
        compiler_params=pltpu.CompilerParams(vmem_limit_bytes=20 << 20),
        cost_estimate=pl.CostEstimate(
            flops=6 * 1024 * channels * channels, bytes_accessed=12 << 20, transcendentals=0
        ),
    )(where, *arrays)
    return [o.reshape(12 * block, channels) for o in out]


def back_kernel(where, before, here, after, weight, slope, gated, grad, lend, acc):
    def product(value, k):
        return lax.dot_general(
            value, weight[k], (((1,), (1,)), ((), ())), preferred_element_type=F32
        )

    lend[1] = here[...]
    lend[3] = gated[...]
    none = jnp.zeros(here.shape, here.dtype)
    acc[...] = product(here[...], 1)

    @pl.when(where[0] == 15)
    def _():
        lend[0] = none

    @pl.when(where[0] < 15)
    def _():
        lend[0] = after[...]
        acc[...] += product(after[...], 0)

    @pl.when(where[0] == 0)
    def _():
        lend[2] = none

    @pl.when(where[0] > 0)
    def _():
        lend[2] = before[...]
        acc[...] += product(before[...], 2)

    grad[...] = (acc[...].astype(BF16).astype(F32) * slope[...]).astype(BF16)


def back(where, before, here, after, weight, slope, gated):
    pixels, channels = here.shape

    def whole(array):
        return pl.BlockSpec(array.shape, lambda t, where: (0,) * array.ndim)

    arrays = (before, here, after, weight, slope, gated)
    outs = [
        jax.ShapeDtypeStruct((pixels, channels), BF16),
        jax.ShapeDtypeStruct((4, pixels, channels), BF16),
    ]
    return pl.pallas_call(
        back_kernel,
        out_shape=outs,
        grid_spec=pltpu.PrefetchScalarGridSpec(
            num_scalar_prefetch=1,
            grid=(1,),
            in_specs=[whole(a) for a in arrays],
            out_specs=[whole(o) for o in outs],
            scratch_shapes=[pltpu.VMEM((pixels, channels), F32)],
        ),
        compiler_params=pltpu.CompilerParams(vmem_limit_bytes=20 << 20),
        cost_estimate=pl.CostEstimate(
            flops=6 * pixels * channels * channels, bytes_accessed=8 << 20, transcendentals=0
        ),
        name="back",
    )(where, *arrays)


def forward_kernel(turned, weight, gated, slope, acc):
    tap = pl.program_id(0)
    pixels = acc.shape[0]
    start = pl.multiple_of(tap // 3 * WIDTH, WIDTH)
    here = turned[tap % 3, pl.ds(start, pixels), :]
    term = jnp.dot(here, weight[0], preferred_element_type=F32)

    @pl.when(tap == 0)
    def _():
        acc[...] = term

    @pl.when(tap > 0)
    def _():
        acc[...] += term

    @pl.when(tap == 8)
    def _():
        pre_act = acc[...]
        logistic = jax.nn.sigmoid(pre_act)
        gated[...] = (pre_act * logistic).astype(BF16)
        slope[...] = logistic * (1.0 + pre_act * (1.0 - logistic))


def forward(turned, weight):
    pixels = turned.shape[1] - 2 * WIDTH
    channels = turned.shape[2]
    whole = pl.BlockSpec((pixels, channels), lambda t: (0, 0))
    return pl.pallas_call(
        forward_kernel,
        out_shape=[
            jax.ShapeDtypeStruct((pixels, channels), BF16),
            jax.ShapeDtypeStruct((pixels, channels), F32),
        ],
        grid=(9,),
        in_specs=[
            pl.BlockSpec(turned.shape, lambda t: (0, 0, 0)),
            pl.BlockSpec((1, channels, channels), lambda t: (t, 0, 0)),
        ],
        out_specs=[whole, whole],
        scratch_shapes=[pltpu.VMEM((pixels, channels), F32)],
        compiler_params=pltpu.CompilerParams(vmem_limit_bytes=20 << 20),
        cost_estimate=pl.CostEstimate(
            flops=18 * pixels * channels * channels,
            bytes_accessed=12 << 20,
            transcendentals=pixels * channels,
        ),
        name="forward",
    )(turned, weight)


def on_device(latents, cotangent, timesteps, spatial_weight, temporal_weight):
    channels = latents.shape[3]
    pixels = latents.shape[2]
    frames = SIZES["y"] * SIZES["x"]
    block = channels // frames
    cot = cotangent.reshape(pixels, channels)
    core, y_here, x_here = (lax.axis_index(name) for name in ("core", "y", "x"))
    frame = y_here * SIZES["x"] + x_here
    places = dict(
        frame=frame.reshape(1).astype(jnp.int32),
        edge=jnp.stack([core, x_here]).astype(jnp.int32),
        mixed=jnp.stack([core, y_here]).astype(jnp.int32),
        y=[(y_here + j) & 3 for j in range(4)],
        x=[(x_here + j) & 3 for j in range(4)],
        first=jnp.broadcast_to(core == 0, (1, 1, 1)),
        row=frame * block,
    )
    places, cot, latents = lax.optimization_barrier((places, cot, latents))
    cot_prev = lax.ppermute(cot, ("y", "x"), [(f, (f + 1) % frames) for f in range(frames)])
    cot_next = lax.ppermute(cot, ("y", "x"), [((f + 1) % frames, f) for f in range(frames)])

    both = [(0, 1), (1, 0)]
    shifts = embed(timesteps, channels)
    activated = jax.nn.silu(latents.reshape(pixels, channels).astype(F32) + shifts).astype(BF16)

    border = ((0, 0), (WIDTH, WIDTH), (0, 0))
    turned = jnp.concatenate(
        [jnp.pad(shift_cols(activated[None], e - 1), border) for e in range(3)], 0
    )
    turned_far = lax.ppermute(turned, "core", both)
    gated, slope = forward(turned, spatial_weight)
    grad, lend = back(places["frame"], cot_prev, cot, cot_next, temporal_weight, slope, gated)
    grad_far = lax.ppermute(grad, "core", both)
    grad_far, lend = lax.optimization_barrier((grad_far, lend))
    lent = lax.ppermute(lend, "core", both)

    step_of = lambda e: e
    sources = (turned, turned_far, grad, grad_far)
    shares_a = taps(edge_kernel, places["edge"], sources, (step_of, step_of, None, None))
    share_a = shares_a.__getitem__
    opened = ring_open(share_a, "x")
    gate_of = lambda e: 3
    shares_b = taps(
        mixed_kernel,
        places["mixed"],
        sources + (lend, lend, lent, lent),
        (step_of, step_of, None, None, step_of, gate_of, step_of, gate_of),
    )
    opened, shares_b = lax.optimization_barrier((opened, shares_b))
    share_b = shares_b.__getitem__
    opened_b = ring_open(share_b, "y")
    part_a1 = ring_close(share_a, "x", *opened).reshape(4, 3 * block, channels)
    part_b1 = ring_close(share_b, "y", *opened_b).reshape(4, 3 * block, channels)

    def pick(value, axis):
        return lambda j: lax.dynamic_index_in_dim(value, places[axis][j], 0, keepdims=False, allow_negative_indices=False)

    part_a = direct_scatter(pick(part_a1, "y"), "y")
    part_b = direct_scatter(pick(part_b1, "x"), "x")
    part = jnp.concatenate([part_a, part_b], 0)
    part = lax.all_to_all(part.reshape(8, -1, channels), "z", 0, 0)
    part = jnp.sum(part.astype(F32), axis=0).astype(BF16)
    part = lax.all_to_all(jnp.broadcast_to(part[None], (8,) + part.shape), "z", 0, 0)
    mine = part.reshape(6, block, channels)
    other = lax.ppermute(mine, "core", both)
    total = jnp.concatenate(
        [jnp.where(places["first"], mine, other), jnp.where(places["first"], other, mine)], 0
    ).astype(F32)
    squares = jnp.sum(jnp.square(total)).reshape(1, 1, 1) + jnp.zeros((frames, 1, 128), F32)
    squares = lax.all_to_all(squares, ("y", "x"), 0, 0)
    squares = jnp.sum(squares[:, 0, 0])
    factor = clip_factor(squares, channels)
    row_start = places["row"]
    spatial_here = lax.dynamic_slice(spatial_weight, (0, row_start, 0), (9, block, channels), allow_negative_indices=False)
    temporal_here = lax.dynamic_slice(temporal_weight, (0, row_start, 0), (3, block, channels), allow_negative_indices=False)
    new_spatial = spatial_here.astype(F32) - factor * total[:9]
    new_temporal = temporal_here.astype(F32) - factor * total[9:]
    return (new_spatial, new_temporal)


def solution(mesh):
    names = tuple(SIZES)
    grid = Mesh(mesh.devices.reshape(tuple(SIZES.values())), names)
    rows, frame = ("z", "core"), ("y", "x")
    in_specs = (P(rows, frame, None, None), P(rows, frame, None, None), P(rows), P(), P())
    out_specs = (P(None, frame, None), P(None, frame, None))

    return jax.shard_map(
        on_device, mesh=grid, in_specs=in_specs, out_specs=out_specs, check_vma=False
    )
```

profile of v0, /device:TPU:0, one launch (start us, length us, event | category | flops | bytes accessed | tf_op | source)
XLA Modules:
  0.0 138.1 jit_solution(15403632827448034194)
XLA Ops:
  0.8 5.3 %collective-permute-start.2 = (bf16[512,640]{1,0:T(8,128)(2,1)}, bf16[512,640]{1,0:T(8,128)(2,1)S(1)}, u32[]{:S(2)}, u32[]{:S(2)}) collective-permute-start(bf16[512,640]{1,0:T(8,128)(2,1)} %bitcast.49), channel_id=1, source_target_pairs={{1,0},{2,1},{3,2},{4,3},{5,4},{6,5},{7,6},{8,7},{9,8},{10,9},{11,1... | collective-permute-start | bytes 1966088 | tf_op jit(solution)/shard_map/ppermute | solution.py:289
  9.6 1.9 %copy-done.2 = bf16[9,640,640]{2,1,0:T(8,128)(2,1)S(1)} copy-done((bf16[9,640,640]{2,1,0:T(8,128)(2,1)S(1)}, bf16[9,640,640]{2,1,0:T(8,128)(2,1)}, u32[]{:S(2)}) %copy-start.2) | copy-done | bytes 7372824
  11.5 8.3 %forward.1 = (bf16[512,640]{1,0:T(8,128)(2,1)S(1)}, f32[512,640]{1,0:T(8,128)S(1)}) custom-call(bf16[3,640,640]{2,1,0:T(8,128)(2,1)S(1)} %fusion.5.turned, bf16[9,640,640]{2,1,0:T(8,128)(2,1)S(1)} %copy-done.2), custom_call_target="tpu_custom_call" | custom-call | flops 3774873600 | bytes 12582912 | tf_op jit(solution)/shard_map/forward/pallas_call | solution.py:247
  19.9 1.9 %back.1 = (bf16[512,640]{1,0:T(8,128)(2,1)S(1)}, bf16[4,512,640]{2,1,0:T(8,128)(2,1)S(1)}) custom-call(s32[1]{0:T(128)} %bitcast.3.where, bf16[512,640]{1,0:T(8,128)(2,1)S(1)} %collective-permute-done.1.before, bf16[512,640]{1,0:T(8,128)(2,1)S(1)} %bitcast.50, bf16[512,640]{1,0:T(8,128)(2,1)S(1)} %collective-permute-done.2.after, ...), custom_call_target="tpu_custom_call" | custom-call | flops 1258291200 | bytes 8388608 | tf_op jit(solution)/shard_map/back/pallas_call | solution.py:202
  21.9 2.1 %collective-permute-done.3.grad_far = bf16[512,640]{1,0:T(8,128)(2,1)S(1)} collective-permute-done((bf16[512,640]{1,0:T(8,128)(2,1)S(1)}, bf16[512,640]{1,0:T(8,128)(2,1)S(1)}, u32[]{:S(2)}, u32[]{:S(2)}) %collective-permute-start.3) | collective-permute-done | bytes 655392 | tf_op jit(solution)/shard_map/ppermute | solution.py:302
  24.1 5.1 %shard_map.68 = (bf16[4,3,40,640]{3,2,1,0:T(8,128)(2,1)S(1)}, bf16[4,3,40,640]{3,2,1,0:T(8,128)(2,1)S(1)}, bf16[4,3,40,640]{3,2,1,0:T(8,128)(2,1)S(1)}, bf16[4,3,40,640]{3,2,1,0:T(8,128)(2,1)S(1)}) custom-call(s32[2]{0:T(128)S(1)} %get-tuple-element.39.where, bf16[3,640,640]{2,1,0:T(8,128)(2,1)S(1)} %fusion.5.turned, ...), custom_call_target="tpu_custom_call" | custom-call | flops 2516582400 | bytes 12582912 | tf_op jit(solution)/shard_map/pallas_call | solution.py:141
  29.4 3.2 %collective-permute-start.5 = (bf16[240,640]{1,0:T(8,128)(2,1)S(1)}, bf16[240,640]{1,0:T(8,128)(2,1)S(1)}, u32[]{:S(2)}, u32[]{:S(2)}) collective-permute-start(bf16[240,640]{1,0:T(8,128)(2,1)S(1)} %bitcast.63), channel_id=1, source_target_pairs={{0,3},{1,0},{2,1},{3,2},{4,7},{5,4},{6,5},{7,6},{8,11},{9,8},{10,9... | collective-permute-start | bytes 921608 | tf_op jit(solution)/shard_map/ppermute | solution.py:34
  32.7 4.6 %shard_map.69 = (bf16[4,3,40,640]{3,2,1,0:T(8,128)(2,1)S(1)}, bf16[4,3,40,640]{3,2,1,0:T(8,128)(2,1)S(1)}, bf16[4,3,40,640]{3,2,1,0:T(8,128)(2,1)S(1)}, bf16[4,3,40,640]{3,2,1,0:T(8,128)(2,1)S(1)}) custom-call(s32[2]{0:T(128)S(1)} %get-tuple-element.51.where, bf16[3,640,640]{2,1,0:T(8,128)(2,1)S(1)} %fusion.5.turned, ...), custom_call_target="tpu_custom_call" | custom-call | flops 2516582400 | bytes 12582912 | tf_op jit(solution)/shard_map/pallas_call | solution.py:141
  37.3 2.8 %collective-permute-done.4 = bf16[240,640]{1,0:T(8,128)(2,1)S(1)} collective-permute-done((bf16[240,640]{1,0:T(8,128)(2,1)S(1)}, bf16[240,640]{1,0:T(8,128)(2,1)S(1)}, u32[]{:S(2)}, u32[]{:S(2)}) %collective-permute-start.4) | collective-permute-done | bytes 307232 | tf_op jit(solution)/shard_map/ppermute | solution.py:34
  43.2 2.2 %collective-permute-start.8 = (bf16[480,640]{1,0:T(8,128)(2,1)S(1)}, bf16[480,640]{1,0:T(8,128)(2,1)S(1)}, u32[]{:S(2)}, u32[]{:S(2)}) collective-permute-start(bf16[480,640]{1,0:T(8,128)(2,1)S(1)} %pad_maximum_fusion.1), channel_id=1, source_target_pairs={{0,3},{1,0},{2,1},{3,2},{4,7},{5,4},{6,5},{7,6},{8,11},{9,8},{10,9... | collective-permute-start | bytes 1843208 | tf_op jit(solution)/shard_map/ppermute | solution.py:34
  45.4 2.0 %collective-permute-start.14 = (bf16[240,640]{1,0:T(8,128)(2,1)S(1)}, bf16[240,640]{1,0:T(8,128)(2,1)S(1)}, u32[]{:S(2)}, u32[]{:S(2)}) collective-permute-start(bf16[240,640]{1,0:T(8,128)(2,1)S(1)} %get-tuple-element.87), channel_id=1, source_target_pairs={{0,12},{4,0},{8,4},{12,8},{1,13},{5,1},{9,5},{13,9},{2,14},{6,2},{... | collective-permute-start | bytes 921608 | tf_op jit(solution)/shard_map/ppermute | solution.py:34
  47.4 3.7 %collective-permute-done.12 = bf16[240,640]{1,0:T(8,128)(2,1)S(1)} collective-permute-done((bf16[240,640]{1,0:T(8,128)(2,1)S(1)}, bf16[240,640]{1,0:T(8,128)(2,1)S(1)}, u32[]{:S(2)}, u32[]{:S(2)}) %collective-permute-start.12) | collective-permute-done | bytes 307232 | tf_op jit(solution)/shard_map/ppermute | solution.py:34
  51.7 2.0 %collective-permute-done.14 = bf16[240,640]{1,0:T(8,128)(2,1)S(1)} collective-permute-done((bf16[240,640]{1,0:T(8,128)(2,1)S(1)}, bf16[240,640]{1,0:T(8,128)(2,1)S(1)}, u32[]{:S(2)}, u32[]{:S(2)}) %collective-permute-start.14) | collective-permute-done | bytes 307232 | tf_op jit(solution)/shard_map/ppermute | solution.py:34
  53.8 2.9 %collective-permute-start.15 = (bf16[480,640]{1,0:T(8,128)(2,1)S(1)}, bf16[480,640]{1,0:T(8,128)(2,1)S(1)}, u32[]{:S(2)}, u32[]{:S(2)}) collective-permute-start(bf16[480,640]{1,0:T(8,128)(2,1)S(1)} %pad_maximum_fusion.3), channel_id=1, source_target_pairs={{0,12},{4,0},{8,4},{12,8},{1,13},{5,1},{9,5},{13,9},{2,14},{6,2},{... | collective-permute-start | bytes 1843208 | tf_op jit(solution)/shard_map/ppermute | solution.py:34
  62.0 9.6 %collective-permute-done.13 = bf16[480,640]{1,0:T(8,128)(2,1)S(1)} collective-permute-done((bf16[480,640]{1,0:T(8,128)(2,1)S(1)}, bf16[480,640]{1,0:T(8,128)(2,1)S(1)}, u32[]{:S(2)}, u32[]{:S(2)}) %collective-permute-start.13) | collective-permute-done | bytes 614432 | tf_op jit(solution)/shard_map/ppermute | solution.py:34
  73.1 2.1 %collective-permute-start.17 = (bf16[120,640]{1,0:T(8,128)(2,1)S(1)}, bf16[120,640]{1,0:T(8,128)(2,1)S(1)}, u32[]{:S(2)}, u32[]{:S(2)}) collective-permute-start(bf16[120,640]{1,0:T(8,128)(2,1)S(1)} %get-tuple-element.85), channel_id=1, source_target_pairs={{0,3},{1,0},{2,1},{3,2},{4,7},{5,4},{6,5},{7,6},{8,11},{9,8},{10,9... | collective-permute-start | bytes 460808 | tf_op jit(solution)/shard_map/ppermute | solution.py:34
  75.2 1.9 %collective-permute-start.18 = (bf16[120,640]{1,0:T(8,128)(2,1)S(1)}, bf16[120,640]{1,0:T(8,128)(2,1)S(1)}, u32[]{:S(2)}, u32[]{:S(2)}) collective-permute-start(bf16[120,640]{1,0:T(8,128)(2,1)S(1)} %get-tuple-element.84), channel_id=1, source_target_pairs={{0,2},{1,3},{2,0},{3,1},{4,6},{5,7},{6,4},{7,5},{8,10},{9,11},{10,... | collective-permute-start | bytes 460808 | tf_op jit(solution)/shard_map/ppermute | solution.py:34
  78.4 3.5 %collective-permute-done.18 = bf16[120,640]{1,0:T(8,128)(2,1)S(1)} collective-permute-done((bf16[120,640]{1,0:T(8,128)(2,1)S(1)}, bf16[120,640]{1,0:T(8,128)(2,1)S(1)}, u32[]{:S(2)}, u32[]{:S(2)}) %collective-permute-start.18) | collective-permute-done | bytes 153632 | tf_op jit(solution)/shard_map/ppermute | solution.py:34
  82.1 19.5 %all_to_all.15 = bf16[8,30,640]{2,1,0:T(8,128)(2,1)S(1)} all-to-all(bf16[8,30,640]{2,1,0:T(8,128)(2,1)S(1)} %reshape.175), channel_id=1, replica_groups=mesh['z'=8,'core'=2,'y'=4,'x'=4] {'z'}, dimensions={0} | all-to-all | bytes 614400 | tf_op jit(solution)/shard_map/all_to_all | solution.py:330
  101.7 13.6 %all_to_all.16 = bf16[8,30,640]{2,1,0:T(8,128)(2,1)S(1)} all-to-all(bf16[8,30,640]{2,1,0:T(8,128)(2,1)S(1)} %broadcast_in_dim.51), channel_id=1, replica_groups=mesh['z'=8,'core'=2,'y'=4,'x'=4] {'z'}, dimensions={0} | all-to-all | bytes 614400 | tf_op jit(solution)/shard_map/all_to_all | solution.py:332
  119.3 5.8 %all-to-all-start.2 = ((f32[16,1,128]{2,1,0:T(1,128)}), f32[16,1,128]{2,1,0:T(1,128)S(1)}, u32[]{:S(2)}, u32[]{:S(2)}) async-start(f32[16,1,128]{2,1,0:T(1,128)} %add.153), calls=%async_computation.2 | async-start | bytes 16384 | tf_op jit(solution)/shard_map/all_to_all | solution.py:339
  126.2 6.4 %all-to-all-done.2 = f32[16,1,128]{2,1,0:T(1,128)S(1)} async-done(((f32[16,1,128]{2,1,0:T(1,128)}), f32[16,1,128]{2,1,0:T(1,128)S(1)}, u32[]{:S(2)}, u32[]{:S(2)}) %all-to-all-start.2) | async-done | bytes 8224 | tf_op jit(solution)/shard_map/all_to_all | solution.py:339
  133.9 1.7 %fusion.17 = f32[3,40,640]{2,1,0:T(8,128)} fusion(f32[12,40,640]{2,1,0:T(8,128)} %maximum_convert_fusion, f32[]{:T(128)S(6)} %min_shard_map.3, bf16[3,640,640]{2,1,0:T(8,128)(2,1)S(1)} %copy-done, s32[]{:T(128)S(6)} %mul.56), kind=kLoop, calls=%fused_computation.38 | loop fusion | flops 230400 | bytes 768008 | tf_op jit(solution)/shard_map/sub | solution.py:346
  135.7 2.4 %fusion.14 = f32[9,40,640]{2,1,0:T(8,128)} fusion(f32[12,40,640]{2,1,0:T(8,128)} %maximum_convert_fusion, f32[]{:T(128)S(6)} %min_shard_map.3, bf16[9,640,640]{2,1,0:T(8,128)(2,1)} %weight.2, s32[]{:T(128)S(6)} %mul.56), kind=kLoop, calls=%fused_computation.23 | loop fusion | flops 691200 | bytes 2304008 | tf_op jit(solution)/shard_map/sub | solution.py:345
  (71 shorter events, 21.4 us)
Async XLA Ops:
  0.7 19.1 %collective-permute-start.1 = (bf16[512,640]{1,0:T(8,128)(2,1)}, bf16[512,640]{1,0:T(8,128)(2,1)S(1)}, u32[]{:S(2)}, u32[]{:S(2)}) collective-permute-start(bf16[512,640]{1,0:T(8,128)(2,1)} %bitcast.48), channel_id=1, source_target_pairs={{0,1},{1,2},{2,3},{3,4},{4,5},{5,6},{6,7},{7,8},{8,9},{9,10},{10,1... | collective-permute-start | bytes 1966088 | tf_op jit(solution)/shard_map/ppermute | solution.py:288
  0.8 19.1 %collective-permute-start.2 = (bf16[512,640]{1,0:T(8,128)(2,1)}, bf16[512,640]{1,0:T(8,128)(2,1)S(1)}, u32[]{:S(2)}, u32[]{:S(2)}) collective-permute-start(bf16[512,640]{1,0:T(8,128)(2,1)} %bitcast.49), channel_id=1, source_target_pairs={{1,0},{2,1},{3,2},{4,3},{5,4},{6,5},{7,6},{8,7},{9,8},{10,9},{11,1... | collective-permute-start | bytes 1966088 | tf_op jit(solution)/shard_map/ppermute | solution.py:289
  8.4 3.1 %copy-start.2 = (bf16[9,640,640]{2,1,0:T(8,128)(2,1)S(1)}, bf16[9,640,640]{2,1,0:T(8,128)(2,1)}, u32[]{:S(2)}) copy-start(bf16[9,640,640]{2,1,0:T(8,128)(2,1)} %weight.2) | copy-start | bytes 22118404
  9.4 10.4 %copy-start.1 = (bf16[1,1,512,640]{3,2,1,0:T(8,128)(2,1)S(1)}, bf16[1,1,512,640]{3,2,1,0:T(8,128)(2,1)}, u32[]{:S(2)}) copy-start(bf16[1,1,512,640]{3,2,1,0:T(8,128)(2,1)} %param.6) | copy-start | bytes 1966084
  9.5 14.6 %collective-permute-start = (bf16[3,640,640]{2,1,0:T(8,128)(2,1)S(1)}, bf16[3,640,640]{2,1,0:T(8,128)(2,1)S(1)}, u32[]{:S(2)}, u32[]{:S(2)}) collective-permute-start(bf16[3,640,640]{2,1,0:T(8,128)(2,1)S(1)} %fusion.5.turned), channel_id=1, source_target_pairs={{0,16},{16,0},{1,17},{17,1},{2,18},{18,2},{3,19},{19,3},{4,20},{20... | collective-permute-start | bytes 7372808 | tf_op jit(solution)/shard_map/ppermute | solution.py:299
  11.5 8.4 %copy-start = (bf16[3,640,640]{2,1,0:T(8,128)(2,1)S(1)}, bf16[3,640,640]{2,1,0:T(8,128)(2,1)}, u32[]{:S(2)}) copy-start(bf16[3,640,640]{2,1,0:T(8,128)(2,1)} %weight.3) | copy-start | bytes 7372804
  21.8 2.2 %collective-permute-start.3 = (bf16[512,640]{1,0:T(8,128)(2,1)S(1)}, bf16[512,640]{1,0:T(8,128)(2,1)S(1)}, u32[]{:S(2)}, u32[]{:S(2)}) collective-permute-start(bf16[512,640]{1,0:T(8,128)(2,1)S(1)} %get-tuple-element.45.grad), channel_id=1, source_target_pairs={{0,16},{16,0},{1,17},{17,1},{2,18},{18,2},{3,19},{19,3},{4,20},{20... | collective-permute-start | bytes 1966088 | tf_op jit(solution)/shard_map/ppermute | solution.py:302
  24.0 8.8 %collective-permute-start.6 = (bf16[4,512,640]{2,1,0:T(8,128)(2,1)S(1)}, bf16[4,512,640]{2,1,0:T(8,128)(2,1)S(1)}, u32[]{:S(2)}, u32[]{:S(2)}) collective-permute-start(bf16[4,512,640]{2,1,0:T(8,128)(2,1)S(1)} %get-tuple-element.52.cots.gate), channel_id=1, source_target_pairs={{0,16},{16,0},{1,17},{17,1},{2,18},{18,2},{3,19},{19,3},{4,20},{20... | collective-permute-start | bytes 7864328 | tf_op jit(solution)/shard_map/ppermute | solution.py:304
  29.3 10.8 %collective-permute-start.4 = (bf16[240,640]{1,0:T(8,128)(2,1)S(1)}, bf16[240,640]{1,0:T(8,128)(2,1)S(1)}, u32[]{:S(2)}, u32[]{:S(2)}) collective-permute-start(bf16[240,640]{1,0:T(8,128)(2,1)S(1)} %bitcast.64), channel_id=1, source_target_pairs={{0,1},{1,2},{2,3},{3,0},{4,5},{5,6},{6,7},{7,4},{8,9},{9,10},{10,1... | collective-permute-start | bytes 921608 | tf_op jit(solution)/shard_map/ppermute | solution.py:34
  29.4 10.8 %collective-permute-start.5 = (bf16[240,640]{1,0:T(8,128)(2,1)S(1)}, bf16[240,640]{1,0:T(8,128)(2,1)S(1)}, u32[]{:S(2)}, u32[]{:S(2)}) collective-permute-start(bf16[240,640]{1,0:T(8,128)(2,1)S(1)} %bitcast.63), channel_id=1, source_target_pairs={{0,3},{1,0},{2,1},{3,2},{4,7},{5,4},{6,5},{7,6},{8,11},{9,8},{10,9... | collective-permute-start | bytes 921608 | tf_op jit(solution)/shard_map/ppermute | solution.py:34
  40.3 16.6 %collective-permute-start.7 = (bf16[480,640]{1,0:T(8,128)(2,1)S(1)}, bf16[480,640]{1,0:T(8,128)(2,1)S(1)}, u32[]{:S(2)}, u32[]{:S(2)}) collective-permute-start(bf16[480,640]{1,0:T(8,128)(2,1)S(1)} %pad_maximum_fusion), channel_id=1, source_target_pairs={{0,1},{1,2},{2,3},{3,0},{4,5},{5,6},{6,7},{7,4},{8,9},{9,10},{10,1... | collective-permute-start | bytes 1843208 | tf_op jit(solution)/shard_map/ppermute | solution.py:34
  41.4 9.7 %collective-permute-start.12 = (bf16[240,640]{1,0:T(8,128)(2,1)S(1)}, bf16[240,640]{1,0:T(8,128)(2,1)S(1)}, u32[]{:S(2)}, u32[]{:S(2)}) collective-permute-start(bf16[240,640]{1,0:T(8,128)(2,1)S(1)} %get-tuple-element.86), channel_id=1, source_target_pairs={{0,4},{4,8},{8,12},{12,0},{1,5},{5,9},{9,13},{13,1},{2,6},{6,10},{... | collective-permute-start | bytes 921608 | tf_op jit(solution)/shard_map/ppermute | solution.py:34
  43.2 14.8 %collective-permute-start.8 = (bf16[480,640]{1,0:T(8,128)(2,1)S(1)}, bf16[480,640]{1,0:T(8,128)(2,1)S(1)}, u32[]{:S(2)}, u32[]{:S(2)}) collective-permute-start(bf16[480,640]{1,0:T(8,128)(2,1)S(1)} %pad_maximum_fusion.1), channel_id=1, source_target_pairs={{0,3},{1,0},{2,1},{3,2},{4,7},{5,4},{6,5},{7,6},{8,11},{9,8},{10,9... | collective-permute-start | bytes 1843208 | tf_op jit(solution)/shard_map/ppermute | solution.py:34
  45.4 8.2 %collective-permute-start.14 = (bf16[240,640]{1,0:T(8,128)(2,1)S(1)}, bf16[240,640]{1,0:T(8,128)(2,1)S(1)}, u32[]{:S(2)}, u32[]{:S(2)}) collective-permute-start(bf16[240,640]{1,0:T(8,128)(2,1)S(1)} %get-tuple-element.87), channel_id=1, source_target_pairs={{0,12},{4,0},{8,4},{12,8},{1,13},{5,1},{9,5},{13,9},{2,14},{6,2},{... | collective-permute-start | bytes 921608 | tf_op jit(solution)/shard_map/ppermute | solution.py:34
  51.2 20.4 %collective-permute-start.13 = (bf16[480,640]{1,0:T(8,128)(2,1)S(1)}, bf16[480,640]{1,0:T(8,128)(2,1)S(1)}, u32[]{:S(2)}, u32[]{:S(2)}) collective-permute-start(bf16[480,640]{1,0:T(8,128)(2,1)S(1)} %pad_maximum_fusion.2), channel_id=1, source_target_pairs={{0,4},{4,8},{8,12},{12,0},{1,5},{5,9},{9,13},{13,1},{2,6},{6,10},{... | collective-permute-start | bytes 1843208 | tf_op jit(solution)/shard_map/ppermute | solution.py:34
  53.8 17.8 %collective-permute-start.15 = (bf16[480,640]{1,0:T(8,128)(2,1)S(1)}, bf16[480,640]{1,0:T(8,128)(2,1)S(1)}, u32[]{:S(2)}, u32[]{:S(2)}) collective-permute-start(bf16[480,640]{1,0:T(8,128)(2,1)S(1)} %pad_maximum_fusion.3), channel_id=1, source_target_pairs={{0,12},{4,0},{8,4},{12,8},{1,13},{5,1},{9,5},{13,9},{2,14},{6,2},{... | collective-permute-start | bytes 1843208 | tf_op jit(solution)/shard_map/ppermute | solution.py:34
  58.3 16.9 %collective-permute-start.10 = (bf16[120,640]{1,0:T(8,128)(2,1)S(1)}, bf16[120,640]{1,0:T(8,128)(2,1)S(1)}, u32[]{:S(2)}, u32[]{:S(2)}) collective-permute-start(bf16[120,640]{1,0:T(8,128)(2,1)S(1)} %get-tuple-element.78), channel_id=1, source_target_pairs={{0,12},{4,0},{8,4},{12,8},{1,13},{5,1},{9,5},{13,9},{2,14},{6,2},{... | collective-permute-start | bytes 460808 | tf_op jit(solution)/shard_map/ppermute | solution.py:34
  60.1 17.0 %collective-permute-start.11 = (bf16[120,640]{1,0:T(8,128)(2,1)S(1)}, bf16[120,640]{1,0:T(8,128)(2,1)S(1)}, u32[]{:S(2)}, u32[]{:S(2)}) collective-permute-start(bf16[120,640]{1,0:T(8,128)(2,1)S(1)} %get-tuple-element.77), channel_id=1, source_target_pairs={{0,8},{4,12},{8,0},{12,4},{1,9},{5,13},{9,1},{13,5},{2,10},{6,14},... | collective-permute-start | bytes 460808 | tf_op jit(solution)/shard_map/ppermute | solution.py:34
  61.8 15.3 %collective-permute-start.9 = (bf16[120,640]{1,0:T(8,128)(2,1)S(1)}, bf16[120,640]{1,0:T(8,128)(2,1)S(1)}, u32[]{:S(2)}, u32[]{:S(2)}) collective-permute-start(bf16[120,640]{1,0:T(8,128)(2,1)S(1)} %get-tuple-element.76), channel_id=1, source_target_pairs={{0,4},{4,8},{8,12},{12,0},{1,5},{5,9},{9,13},{13,1},{2,6},{6,10},{... | collective-permute-start | bytes 460808 | tf_op jit(solution)/shard_map/ppermute | solution.py:34
  71.9 6.5 %collective-permute-start.16 = (bf16[120,640]{1,0:T(8,128)(2,1)S(1)}, bf16[120,640]{1,0:T(8,128)(2,1)S(1)}, u32[]{:S(2)}, u32[]{:S(2)}) collective-permute-start(bf16[120,640]{1,0:T(8,128)(2,1)S(1)} %get-tuple-element.83), channel_id=1, source_target_pairs={{0,1},{1,2},{2,3},{3,0},{4,5},{5,6},{6,7},{7,4},{8,9},{9,10},{10,1... | collective-permute-start | bytes 460808 | tf_op jit(solution)/shard_map/ppermute | solution.py:34
  73.1 5.2 %collective-permute-start.17 = (bf16[120,640]{1,0:T(8,128)(2,1)S(1)}, bf16[120,640]{1,0:T(8,128)(2,1)S(1)}, u32[]{:S(2)}, u32[]{:S(2)}) collective-permute-start(bf16[120,640]{1,0:T(8,128)(2,1)S(1)} %get-tuple-element.85), channel_id=1, source_target_pairs={{0,3},{1,0},{2,1},{3,2},{4,7},{5,4},{6,5},{7,6},{8,11},{9,8},{10,9... | collective-permute-start | bytes 460808 | tf_op jit(solution)/shard_map/ppermute | solution.py:34
  75.2 6.7 %collective-permute-start.18 = (bf16[120,640]{1,0:T(8,128)(2,1)S(1)}, bf16[120,640]{1,0:T(8,128)(2,1)S(1)}, u32[]{:S(2)}, u32[]{:S(2)}) collective-permute-start(bf16[120,640]{1,0:T(8,128)(2,1)S(1)} %get-tuple-element.84), channel_id=1, source_target_pairs={{0,2},{1,3},{2,0},{3,1},{4,6},{5,7},{6,4},{7,5},{8,10},{9,11},{10,... | collective-permute-start | bytes 460808 | tf_op jit(solution)/shard_map/ppermute | solution.py:34
  115.3 1.7 %collective-permute-start.19 = (bf16[6,40,640]{2,1,0:T(8,128)(2,1)S(1)}, bf16[6,40,640]{2,1,0:T(8,128)(2,1)S(1)}, u32[]{:S(2)}, u32[]{:S(2)}) collective-permute-start(bf16[6,40,640]{2,1,0:T(8,128)(2,1)S(1)} %reshape.176), channel_id=1, source_target_pairs={{0,16},{16,0},{1,17},{17,1},{2,18},{18,2},{3,19},{19,3},{4,20},{20... | collective-permute-start | bytes 921608 | tf_op jit(solution)/shard_map/ppermute | solution.py:334
  119.3 13.3 %all-to-all-start.2 = ((f32[16,1,128]{2,1,0:T(1,128)}), f32[16,1,128]{2,1,0:T(1,128)S(1)}, u32[]{:S(2)}, u32[]{:S(2)}) async-start(f32[16,1,128]{2,1,0:T(1,128)} %add.153), calls=%async_computation.2 | async-start | bytes 16384 | tf_op jit(solution)/shard_map/all_to_all | solution.py:339
where the time goes:
time: 140 us; the launch traced here: 138 us
  waiting for transfers between devices  34.2 us (24%)
  starting transfers between devices  33.8 us (24%)
  blocking collectives  33 us (24%)
  Pallas kernels  19.9 us (14%)
  other arithmetic  10.8 us (8%)
  local copies, waits for them, and re-layouts  3.98 us (3%)
  between operations  2.36 us (2%)
    ppermute x14, waiting for transfers between devices, hop(): lax.ppermute(value, axis, [(i, (i + step) % size) for i in range(size)])  24.1 us
    ppermute x14, starting transfers between devices, hop(): lax.ppermute(value, axis, [(i, (i + step) % size) for i in range(size)])  22.3 us
    all_to_all x1, blocking collectives, on_device(): part = lax.all_to_all(part.reshape(8, -1, channels), 'z', 0, 0)  19.5 us
    all_to_all x1, blocking collectives, on_device(): lax.all_to_all(jnp.broadcast_to(part[None], (8,) + part.shape), 'z', 0, 0)  13.6 us
    pallas_call x2, Pallas kernels, taps(): pl.pallas_call(kernel, out_shape=[share] * 4, grid_spec=pltpu.PrefetchSca...  9.67 us
    pallas_call x1, Pallas kernels, forward(): pl.pallas_call(forward_kernel, out_shape=[jax.ShapeDtypeStruct((pixels, c...  8.33 us
    all_to_all x1, waiting for transfers between devices, on_device(): squares = lax.all_to_all(squares, ('y', 'x'), 0, 0)  6.38 us
    all_to_all x1, starting transfers between devices, on_device(): squares = lax.all_to_all(squares, ('y', 'x'), 0, 0)  5.77 us
  transfers between devices with their start and end apart: 21, of which 11 were waited for; matrix products, arithmetic and copies ran while one was open for 4% of the time, Pallas kernels for 14%

commit v1 on v0

--- a/solution.py
+++ b/solution.py
@@ -267,6 +267,49 @@
     )(turned, weight)
 
 
+def squares_kernel(mine, other, out):
+    total = jnp.zeros(mine.shape[1:], F32)
+    for tap in range(mine.shape[0]):
+        total = total + jnp.square(mine[tap].astype(F32)) + jnp.square(other[tap].astype(F32))
+    total = jnp.sum(jnp.sum(total, axis=0, keepdims=True), axis=1, keepdims=True)
+    out[...] = jnp.broadcast_to(total.reshape(1, 1, 1), out.shape)
+
+
+def step_kernel(where, squares, mine, other, spatial, temporal, new_spatial, new_temporal):
+    channels = spatial.shape[2]
+    total = jnp.sum(squares[:, 0, :], axis=0, keepdims=True)[:, :1]
+    factor = clip_factor(total, channels)
+    first = where[0] == 0
+    for tap in range(12):
+        half = tap % 6
+        near, far = (mine, other) if tap < 6 else (other, mine)
+        part = jnp.where(first, near[half].astype(F32), far[half].astype(F32))
+        if tap < 9:
+            new_spatial[tap] = spatial[tap].astype(F32) - factor * part
+        else:
+            new_temporal[tap - 9] = temporal[tap - 9].astype(F32) - factor * part
+
+
+def clipped_step(where, squares, mine, other, spatial, temporal):
+    def whole(array):
+        return pl.BlockSpec(array.shape, lambda t, where: (0,) * array.ndim)
+
+    arrays = (squares, mine, other, spatial, temporal)
+    outs = [jax.ShapeDtypeStruct(a.shape, F32) for a in (spatial, temporal)]
+    return pl.pallas_call(
+        step_kernel,
+        out_shape=outs,
+        grid_spec=pltpu.PrefetchScalarGridSpec(
+            num_scalar_prefetch=1,
+            grid=(1,),
+            in_specs=[whole(a) for a in arrays],
+            out_specs=[whole(o) for o in outs],
+        ),
+        compiler_params=pltpu.CompilerParams(vmem_limit_bytes=20 << 20),
+        name="step",
+    )(where, *arrays)
+
+
 def on_device(latents, cotangent, timesteps, spatial_weight, temporal_weight):
     channels = latents.shape[3]
     pixels = latents.shape[2]
@@ -281,7 +324,6 @@
         mixed=jnp.stack([core, y_here]).astype(jnp.int32),
         y=[(y_here + j) & 3 for j in range(4)],
         x=[(x_here + j) & 3 for j in range(4)],
-        first=jnp.broadcast_to(core == 0, (1, 1, 1)),
         row=frame * block,
     )
     places, cot, latents = lax.optimization_barrier((places, cot, latents))
@@ -315,9 +357,18 @@
         sources + (lend, lend, lent, lent),
         (step_of, step_of, None, None, step_of, gate_of, step_of, gate_of),
     )
-    opened, shares_b = lax.optimization_barrier((opened, shares_b))
     share_b = shares_b.__getitem__
     opened_b = ring_open(share_b, "y")
+    row_start = places["row"]
+    spatial_here = lax.dynamic_slice(
+        spatial_weight, (0, row_start, 0), (9, block, channels), allow_negative_indices=False
+    )
+    temporal_here = lax.dynamic_slice(
+        temporal_weight, (0, row_start, 0), (3, block, channels), allow_negative_indices=False
+    )
+    opened_b, spatial_here, temporal_here = lax.optimization_barrier(
+        (opened_b, spatial_here, temporal_here)
+    )
     part_a1 = ring_close(share_a, "x", *opened).reshape(4, 3 * block, channels)
     part_b1 = ring_close(share_b, "y", *opened_b).reshape(4, 3 * block, channels)
 
@@ -332,19 +383,14 @@
     part = lax.all_to_all(jnp.broadcast_to(part[None], (8,) + part.shape), "z", 0, 0)
     mine = part.reshape(6, block, channels)
     other = lax.ppermute(mine, "core", both)
-    total = jnp.concatenate(
-        [jnp.where(places["first"], mine, other), jnp.where(places["first"], other, mine)], 0
-    ).astype(F32)
-    squares = jnp.sum(jnp.square(total)).reshape(1, 1, 1) + jnp.zeros((frames, 1, 128), F32)
+    squares = pl.pallas_call(
+        squares_kernel,
+        out_shape=jax.ShapeDtypeStruct((frames, 1, 128), F32),
+        compiler_params=pltpu.CompilerParams(vmem_limit_bytes=20 << 20),
+        name="squares",
+    )(mine, other)
     squares = lax.all_to_all(squares, ("y", "x"), 0, 0)
-    squares = jnp.sum(squares[:, 0, 0])
-    factor = clip_factor(squares, channels)
-    row_start = places["row"]
-    spatial_here = lax.dynamic_slice(spatial_weight, (0, row_start, 0), (9, block, channels), allow_negative_indices=False)
-    temporal_here = lax.dynamic_slice(temporal_weight, (0, row_start, 0), (3, block, channels), allow_negative_indices=False)
-    new_spatial = spatial_here.astype(F32) - factor * total[:9]
-    new_temporal = temporal_here.astype(F32) - factor * total[9:]
-    return (new_spatial, new_temporal)
+    return clipped_step(places["edge"], squares, mine, other, spatial_here, temporal_here)
 
 
 def solution(mesh):

time: 140 us -> 145 us (1.036)
  blocking collectives: 33 us -> 43.3 us
  waiting for transfers between devices: 34.2 us -> 44.4 us
  starting transfers between devices: 33.8 us -> 26.2 us
  other arithmetic: 10.8 us -> 4.04 us
  local copies, waits for them, and re-layouts: 3.98 us -> 1.9 us
  Pallas kernels: 19.9 us -> 21.9 us
    all_to_all x0 -> x1, blocking collectives: none -> 10.7 us  [on_device(): squares = lax.all_to_all(squares, ('y', 'x'), 0, 0)]
    ppermute x14, waiting for transfers between devices: 24.1 us -> 34.8 us  [hop(): lax.ppermute(value, axis, [(i, (i + step) % size) for i in range(size)])]
    all_to_all x1 -> x0, waiting for transfers between devices: 6.38 us -> none  [on_device(): squares = lax.all_to_all(squares, ('y', 'x'), 0, 0)]
    ppermute x1, waiting for transfers between devices: 0.01 us -> 5.92 us  [on_device(): lax.ppermute(cot, ('y', 'x'), [(f, (f + 1) % frames) for f in range(frame...]
    all_to_all x1 -> x0, starting transfers between devices: 5.77 us -> none  [on_device(): squares = lax.all_to_all(squares, ('y', 'x'), 0, 0)]
    sub x2 -> x0, other arithmetic: 4.16 us -> none  [the longest x1 2.41 us: on_device(): new_spatial = spatial_here.astype(F32) - factor * total[:9]]
    pallas_call x0 -> x2, Pallas kernels: none -> 1.99 us  [the longest x1 1.8 us: clipped_step(): pl.pallas_call(step_kernel, out_shape=outs, grid_spec=pltpu.PrefetchScala...]
    ppermute x14, starting transfers between devices: 22.3 us -> 20.5 us  [hop(): lax.ppermute(value, axis, [(i, (i + step) % size) for i in range(size)])]
  transfers between devices with their start and end apart: 21 -> 20, of which waited for: 11 -> 10; matrix products, arithmetic and copies ran while one was open for 4% -> 1% of each run, Pallas kernels for 14% -> 14%
where the time goes in v1:
time: 145 us; the launch traced here: 143 us
  waiting for transfers between devices  44.4 us (31%)
  blocking collectives  43.3 us (30%)
  starting transfers between devices  26.2 us (18%)
  Pallas kernels  21.9 us (15%)
  other arithmetic  4.04 us (3%)
  local copies, waits for them, and re-layouts  1.9 us (1%)
  between operations  1.64 us (1%)
    ppermute x14, waiting for transfers between devices, hop(): lax.ppermute(value, axis, [(i, (i + step) % size) for i in range(size)])  34.8 us
    ppermute x14, starting transfers between devices, hop(): lax.ppermute(value, axis, [(i, (i + step) % size) for i in range(size)])  20.5 us
    all_to_all x1, blocking collectives, on_device(): part = lax.all_to_all(part.reshape(8, -1, channels), 'z', 0, 0)  18.6 us
    all_to_all x1, blocking collectives, on_device(): lax.all_to_all(jnp.broadcast_to(part[None], (8,) + part.shape), 'z', 0, 0)  14 us
    all_to_all x1, blocking collectives, on_device(): squares = lax.all_to_all(squares, ('y', 'x'), 0, 0)  10.7 us
    pallas_call x2, Pallas kernels, taps(): pl.pallas_call(kernel, out_shape=[share] * 4, grid_spec=pltpu.PrefetchSca...  9.68 us
    pallas_call x1, Pallas kernels, forward(): pl.pallas_call(forward_kernel, out_shape=[jax.ShapeDtypeStruct((pixels, c...  8.33 us
    ppermute x1, waiting for transfers between devices, on_device(): lax.ppermute(cot, ('y', 'x'), [(f, (f + 1) % frames) for f in range(frame...  5.92 us
  transfers between devices with their start and end apart: 20, of which 10 were waited for; matrix products, arithmetic and copies ran while one was open for 1% of the time, Pallas kernels for 14%

profile of v1, /device:TPU:0, one launch (start us, length us, event | category | flops | bytes accessed | tf_op | source)
XLA Modules:
  0.0 143.4 jit_solution(10450805177387476834)
XLA Ops:
  5.1 5.3 %collective-permute-start.2 = (bf16[512,640]{1,0:T(8,128)(2,1)S(1)}, bf16[512,640]{1,0:T(8,128)(2,1)S(1)}, u32[]{:S(2)}, u32[]{:S(2)}) collective-permute-start(bf16[512,640]{1,0:T(8,128)(2,1)S(1)} %bitcast.56), channel_id=1, source_target_pairs={{1,0},{2,1},{3,2},{4,3},{5,4},{6,5},{7,6},{8,7},{9,8},{10,9},{11,1... | collective-permute-start | bytes 1966088 | tf_op jit(solution)/shard_map/ppermute | solution.py:331
  10.4 8.3 %forward.1 = (bf16[512,640]{1,0:T(8,128)(2,1)S(1)}, f32[512,640]{1,0:T(8,128)S(1)}) custom-call(bf16[3,640,640]{2,1,0:T(8,128)(2,1)S(1)} %fusion.5.turned, bf16[9,640,640]{2,1,0:T(8,128)(2,1)S(1)} %copy-done.2), custom_call_target="tpu_custom_call" | custom-call | flops 3774873600 | bytes 12582912 | tf_op jit(solution)/shard_map/forward/pallas_call | solution.py:247
  18.8 5.9 %collective-permute-done.1.before = bf16[512,640]{1,0:T(8,128)(2,1)S(1)} collective-permute-done((bf16[512,640]{1,0:T(8,128)(2,1)S(1)}, bf16[512,640]{1,0:T(8,128)(2,1)S(1)}, u32[]{:S(2)}, u32[]{:S(2)}) %collective-permute-start.1) | collective-permute-done | bytes 655392 | tf_op jit(solution)/shard_map/ppermute | solution.py:330
  24.7 1.9 %back.1 = (bf16[512,640]{1,0:T(8,128)(2,1)S(1)}, bf16[4,512,640]{2,1,0:T(8,128)(2,1)S(1)}) custom-call(s32[1]{0:T(128)} %bitcast.2.where, bf16[512,640]{1,0:T(8,128)(2,1)S(1)} %collective-permute-done.1.before, bf16[512,640]{1,0:T(8,128)(2,1)S(1)} %bitcast.57, bf16[512,640]{1,0:T(8,128)(2,1)S(1)} %collective-permute-done.2.after, ...), custom_call_target="tpu_custom_call" | custom-call | flops 1258291200 | bytes 8388608 | tf_op jit(solution)/shard_map/back/pallas_call | solution.py:202
  26.7 2.1 %collective-permute-done.3.grad_far = bf16[512,640]{1,0:T(8,128)(2,1)S(1)} collective-permute-done((bf16[512,640]{1,0:T(8,128)(2,1)S(1)}, bf16[512,640]{1,0:T(8,128)(2,1)S(1)}, u32[]{:S(2)}, u32[]{:S(2)}) %collective-permute-start.3) | collective-permute-done | bytes 655392 | tf_op jit(solution)/shard_map/ppermute | solution.py:344
  29.1 5.1 %shard_map.68 = (bf16[4,3,40,640]{3,2,1,0:T(8,128)(2,1)S(1)}, bf16[4,3,40,640]{3,2,1,0:T(8,128)(2,1)S(1)}, bf16[4,3,40,640]{3,2,1,0:T(8,128)(2,1)S(1)}, bf16[4,3,40,640]{3,2,1,0:T(8,128)(2,1)S(1)}) custom-call(s32[2]{0:T(128)S(1)} %get-tuple-element.34.where, bf16[3,640,640]{2,1,0:T(8,128)(2,1)S(1)} %fusion.5.turned, ...), custom_call_target="tpu_custom_call" | custom-call | flops 2516582400 | bytes 12582912 | tf_op jit(solution)/shard_map/pallas_call | solution.py:141
  34.3 2.1 %collective-permute-start.6 = (bf16[240,640]{1,0:T(8,128)(2,1)S(1)}, bf16[240,640]{1,0:T(8,128)(2,1)S(1)}, u32[]{:S(2)}, u32[]{:S(2)}) collective-permute-start(bf16[240,640]{1,0:T(8,128)(2,1)S(1)} %bitcast.68), channel_id=1, source_target_pairs={{0,3},{1,0},{2,1},{3,2},{4,7},{5,4},{6,5},{7,6},{8,11},{9,8},{10,9... | collective-permute-start | bytes 921608 | tf_op jit(solution)/shard_map/ppermute | solution.py:34
  36.6 7.3 %collective-permute-done.6 = bf16[240,640]{1,0:T(8,128)(2,1)S(1)} collective-permute-done((bf16[240,640]{1,0:T(8,128)(2,1)S(1)}, bf16[240,640]{1,0:T(8,128)(2,1)S(1)}, u32[]{:S(2)}, u32[]{:S(2)}) %collective-permute-start.6) | collective-permute-done | bytes 307232 | tf_op jit(solution)/shard_map/ppermute | solution.py:34
  44.1 3.5 %collective-permute-start.7 = (bf16[480,640]{1,0:T(8,128)(2,1)S(1)}, bf16[480,640]{1,0:T(8,128)(2,1)S(1)}, u32[]{:S(2)}, u32[]{:S(2)}) collective-permute-start(bf16[480,640]{1,0:T(8,128)(2,1)S(1)} %pad_maximum_fusion.1), channel_id=1, source_target_pairs={{0,3},{1,0},{2,1},{3,2},{4,7},{5,4},{6,5},{7,6},{8,11},{9,8},{10,9... | collective-permute-start | bytes 1843208 | tf_op jit(solution)/shard_map/ppermute | solution.py:34
  47.9 4.6 %shard_map.69 = (bf16[4,3,40,640]{3,2,1,0:T(8,128)(2,1)S(1)}, bf16[4,3,40,640]{3,2,1,0:T(8,128)(2,1)S(1)}, bf16[4,3,40,640]{3,2,1,0:T(8,128)(2,1)S(1)}, bf16[4,3,40,640]{3,2,1,0:T(8,128)(2,1)S(1)}) custom-call(s32[2]{0:T(128)S(1)} %get-tuple-element.51.where, bf16[3,640,640]{2,1,0:T(8,128)(2,1)S(1)} %fusion.5.turned, ...), custom_call_target="tpu_custom_call" | custom-call | flops 2516582400 | bytes 12582912 | tf_op jit(solution)/shard_map/pallas_call | solution.py:141
  52.5 1.6 %collective-permute-start.12 = (bf16[240,640]{1,0:T(8,128)(2,1)S(1)}, bf16[240,640]{1,0:T(8,128)(2,1)S(1)}, u32[]{:S(2)}, u32[]{:S(2)}) collective-permute-start(bf16[240,640]{1,0:T(8,128)(2,1)S(1)} %bitcast.69), channel_id=1, source_target_pairs={{0,4},{4,8},{8,12},{12,0},{1,5},{5,9},{9,13},{13,1},{2,6},{6,10},{... | collective-permute-start | bytes 921608 | tf_op jit(solution)/shard_map/ppermute | solution.py:34
  54.1 2.1 %collective-permute-start.13 = (bf16[240,640]{1,0:T(8,128)(2,1)S(1)}, bf16[240,640]{1,0:T(8,128)(2,1)S(1)}, u32[]{:S(2)}, u32[]{:S(2)}) collective-permute-start(bf16[240,640]{1,0:T(8,128)(2,1)S(1)} %bitcast.67), channel_id=1, source_target_pairs={{0,12},{4,0},{8,4},{12,8},{1,13},{5,1},{9,5},{13,9},{2,14},{6,2},{... | collective-permute-start | bytes 921608 | tf_op jit(solution)/shard_map/ppermute | solution.py:34
  56.4 6.5 %collective-permute-done.12 = bf16[240,640]{1,0:T(8,128)(2,1)S(1)} collective-permute-done((bf16[240,640]{1,0:T(8,128)(2,1)S(1)}, bf16[240,640]{1,0:T(8,128)(2,1)S(1)}, u32[]{:S(2)}, u32[]{:S(2)}) %collective-permute-start.12) | collective-permute-done | bytes 307232 | tf_op jit(solution)/shard_map/ppermute | solution.py:34
  63.0 3.1 %collective-permute-start.15 = (bf16[480,640]{1,0:T(8,128)(2,1)S(1)}, bf16[480,640]{1,0:T(8,128)(2,1)S(1)}, u32[]{:S(2)}, u32[]{:S(2)}) collective-permute-start(bf16[480,640]{1,0:T(8,128)(2,1)S(1)} %pad_maximum_fusion.3), channel_id=1, source_target_pairs={{0,12},{4,0},{8,4},{12,8},{1,13},{5,1},{9,5},{13,9},{2,14},{6,2},{... | collective-permute-start | bytes 1843208 | tf_op jit(solution)/shard_map/ppermute | solution.py:34
  66.8 2.0 %collective-permute-start.10 = (bf16[120,640]{1,0:T(8,128)(2,1)S(1)}, bf16[120,640]{1,0:T(8,128)(2,1)S(1)}, u32[]{:S(2)}, u32[]{:S(2)}) collective-permute-start(bf16[120,640]{1,0:T(8,128)(2,1)S(1)} %get-tuple-element.69), channel_id=1, source_target_pairs={{0,8},{4,12},{8,0},{12,4},{1,9},{5,13},{9,1},{13,5},{2,10},{6,14},... | collective-permute-start | bytes 460808 | tf_op jit(solution)/shard_map/ppermute | solution.py:34
  70.9 11.8 %collective-permute-done.15 = bf16[480,640]{1,0:T(8,128)(2,1)S(1)} collective-permute-done((bf16[480,640]{1,0:T(8,128)(2,1)S(1)}, bf16[480,640]{1,0:T(8,128)(2,1)S(1)}, u32[]{:S(2)}, u32[]{:S(2)}) %collective-permute-start.15) | collective-permute-done | bytes 614432 | tf_op jit(solution)/shard_map/ppermute | solution.py:34
  82.7 3.6 %collective-permute-done.14 = bf16[480,640]{1,0:T(8,128)(2,1)S(1)} collective-permute-done((bf16[480,640]{1,0:T(8,128)(2,1)S(1)}, bf16[480,640]{1,0:T(8,128)(2,1)S(1)}, u32[]{:S(2)}, u32[]{:S(2)}) %collective-permute-start.14) | collective-permute-done | bytes 614432 | tf_op jit(solution)/shard_map/ppermute | solution.py:34
  90.4 3.1 %collective-permute-done.18 = bf16[120,640]{1,0:T(8,128)(2,1)S(1)} collective-permute-done((bf16[120,640]{1,0:T(8,128)(2,1)S(1)}, bf16[120,640]{1,0:T(8,128)(2,1)S(1)}, u32[]{:S(2)}, u32[]{:S(2)}) %collective-permute-start.18) | collective-permute-done | bytes 153632 | tf_op jit(solution)/shard_map/ppermute | solution.py:34
  93.5 1.7 %collective-permute-done.17 = bf16[120,640]{1,0:T(8,128)(2,1)S(1)} collective-permute-done((bf16[120,640]{1,0:T(8,128)(2,1)S(1)}, bf16[120,640]{1,0:T(8,128)(2,1)S(1)}, u32[]{:S(2)}, u32[]{:S(2)}) %collective-permute-start.17) | collective-permute-done | bytes 153632 | tf_op jit(solution)/shard_map/ppermute | solution.py:34
  96.2 18.6 %all_to_all.15 = bf16[8,30,640]{2,1,0:T(8,128)(2,1)S(1)} all-to-all(bf16[8,30,640]{2,1,0:T(8,128)(2,1)S(1)} %reshape.171), channel_id=1, replica_groups=mesh['z'=8,'core'=2,'y'=4,'x'=4] {'z'}, dimensions={0} | all-to-all | bytes 614400 | tf_op jit(solution)/shard_map/all_to_all | solution.py:381
  114.9 14.0 %all_to_all.16 = bf16[8,30,640]{2,1,0:T(8,128)(2,1)S(1)} all-to-all(bf16[8,30,640]{2,1,0:T(8,128)(2,1)S(1)} %broadcast_in_dim.32), channel_id=1, replica_groups=mesh['z'=8,'core'=2,'y'=4,'x'=4] {'z'}, dimensions={0} | all-to-all | bytes 614400 | tf_op jit(solution)/shard_map/all_to_all | solution.py:383
  129.1 1.6 %collective-permute-done.19.other = bf16[6,40,640]{2,1,0:T(8,128)(2,1)S(1)} collective-permute-done((bf16[6,40,640]{2,1,0:T(8,128)(2,1)S(1)}, bf16[6,40,640]{2,1,0:T(8,128)(2,1)S(1)}, u32[]{:S(2)}, u32[]{:S(2)}) %collective-permute-start.19) | collective-permute-done | bytes 307232 | tf_op jit(solution)/shard_map/ppermute | solution.py:385
  130.9 10.7 %all_to_all.17.squares = f32[16,1,128]{2,1,0:T(1,128)S(1)} all-to-all(f32[16,1,128]{2,1,0:T(1,128)S(1)} %squares.1), channel_id=1, replica_groups=mesh['z'=8,'core'=2,'y'=4,'x'=4] {'y','x'}, dimensions={0} | all-to-all | bytes 16384 | tf_op jit(solution)/shard_map/all_to_all | solution.py:392
  141.6 1.8 %step.1 = (f32[9,40,640]{2,1,0:T(8,128)}, f32[3,40,640]{2,1,0:T(8,128)}) custom-call(s32[2]{0:T(128)S(1)} %get-tuple-element.34.where, f32[16,1,128]{2,1,0:T(1,128)S(1)} %all_to_all.17.squares, bf16[6,40,640]{2,1,0:T(8,128)(2,1)S(1)} %reshape.172.mine, bf16[6,40,640]{2,1,0:T(8,128)(2,1)S(1)} %collective-permute-done.19.other, ...), custom_call_target="tpu_custom_call" | custom-call | tf_op jit(solution)/shard_map/step/pallas_call | solution.py:299
  (67 shorter events, 13.4 us)
Async XLA Ops:
  3.0 7.4 %copy-start.2 = (bf16[9,640,640]{2,1,0:T(8,128)(2,1)S(1)}, bf16[9,640,640]{2,1,0:T(8,128)(2,1)}, u32[]{:S(2)}) copy-start(bf16[9,640,640]{2,1,0:T(8,128)(2,1)} %weight.2) | copy-start | bytes 22118404
  3.7 1.4 copy-start.1
  4.1 25.0 %collective-permute-start = (bf16[3,640,640]{2,1,0:T(8,128)(2,1)S(1)}, bf16[3,640,640]{2,1,0:T(8,128)(2,1)S(1)}, u32[]{:S(2)}, u32[]{:S(2)}) collective-permute-start(bf16[3,640,640]{2,1,0:T(8,128)(2,1)S(1)} %fusion.5.turned), channel_id=1, source_target_pairs={{0,16},{16,0},{1,17},{17,1},{2,18},{18,2},{3,19},{19,3},{4,20},{20... | collective-permute-start | bytes 7372808 | tf_op jit(solution)/shard_map/ppermute | solution.py:341
  5.1 19.6 %collective-permute-start.1 = (bf16[512,640]{1,0:T(8,128)(2,1)S(1)}, bf16[512,640]{1,0:T(8,128)(2,1)S(1)}, u32[]{:S(2)}, u32[]{:S(2)}) collective-permute-start(bf16[512,640]{1,0:T(8,128)(2,1)S(1)} %bitcast.55), channel_id=1, source_target_pairs={{0,1},{1,2},{2,3},{3,4},{4,5},{5,6},{6,7},{7,8},{8,9},{9,10},{10,1... | collective-permute-start | bytes 1966088 | tf_op jit(solution)/shard_map/ppermute | solution.py:330
  5.1 19.6 %collective-permute-start.2 = (bf16[512,640]{1,0:T(8,128)(2,1)S(1)}, bf16[512,640]{1,0:T(8,128)(2,1)S(1)}, u32[]{:S(2)}, u32[]{:S(2)}) collective-permute-start(bf16[512,640]{1,0:T(8,128)(2,1)S(1)} %bitcast.56), channel_id=1, source_target_pairs={{1,0},{2,1},{3,2},{4,3},{5,4},{6,5},{7,6},{8,7},{9,8},{10,9},{11,1... | collective-permute-start | bytes 1966088 | tf_op jit(solution)/shard_map/ppermute | solution.py:331
  10.4 14.3 %copy-start = (bf16[3,640,640]{2,1,0:T(8,128)(2,1)S(1)}, bf16[3,640,640]{2,1,0:T(8,128)(2,1)}, u32[]{:S(2)}) copy-start(bf16[3,640,640]{2,1,0:T(8,128)(2,1)} %weight.3) | copy-start | bytes 7372804
  26.6 2.2 %collective-permute-start.3 = (bf16[512,640]{1,0:T(8,128)(2,1)S(1)}, bf16[512,640]{1,0:T(8,128)(2,1)S(1)}, u32[]{:S(2)}, u32[]{:S(2)}) collective-permute-start(bf16[512,640]{1,0:T(8,128)(2,1)S(1)} %get-tuple-element.40.grad), channel_id=1, source_target_pairs={{0,16},{16,0},{1,17},{17,1},{2,18},{18,2},{3,19},{19,3},{4,20},{20... | collective-permute-start | bytes 1966088 | tf_op jit(solution)/shard_map/ppermute | solution.py:344
  28.8 19.1 %collective-permute-start.11 = (bf16[4,512,640]{2,1,0:T(8,128)(2,1)S(1)}, bf16[4,512,640]{2,1,0:T(8,128)(2,1)S(1)}, u32[]{:S(2)}, u32[]{:S(2)}) collective-permute-start(bf16[4,512,640]{2,1,0:T(8,128)(2,1)S(1)} %get-tuple-element.52.cots.gate), channel_id=1, source_target_pairs={{0,16},{16,0},{1,17},{17,1},{2,18},{18,2},{3,19},{19,3},{4,20},{20... | collective-permute-start | bytes 7864328 | tf_op jit(solution)/shard_map/ppermute | solution.py:346
  34.3 9.6 %collective-permute-start.6 = (bf16[240,640]{1,0:T(8,128)(2,1)S(1)}, bf16[240,640]{1,0:T(8,128)(2,1)S(1)}, u32[]{:S(2)}, u32[]{:S(2)}) collective-permute-start(bf16[240,640]{1,0:T(8,128)(2,1)S(1)} %bitcast.68), channel_id=1, source_target_pairs={{0,3},{1,0},{2,1},{3,2},{4,7},{5,4},{6,5},{7,6},{8,11},{9,8},{10,9... | collective-permute-start | bytes 921608 | tf_op jit(solution)/shard_map/ppermute | solution.py:34
  36.4 11.1 %collective-permute-start.4 = (bf16[240,640]{1,0:T(8,128)(2,1)S(1)}, bf16[240,640]{1,0:T(8,128)(2,1)S(1)}, u32[]{:S(2)}, u32[]{:S(2)}) collective-permute-start(bf16[240,640]{1,0:T(8,128)(2,1)S(1)} %bitcast.66), channel_id=1, source_target_pairs={{0,1},{1,2},{2,3},{3,0},{4,5},{5,6},{6,7},{7,4},{8,9},{9,10},{10,1... | collective-permute-start | bytes 921608 | tf_op jit(solution)/shard_map/ppermute | solution.py:34
  44.1 22.3 %collective-permute-start.7 = (bf16[480,640]{1,0:T(8,128)(2,1)S(1)}, bf16[480,640]{1,0:T(8,128)(2,1)S(1)}, u32[]{:S(2)}, u32[]{:S(2)}) collective-permute-start(bf16[480,640]{1,0:T(8,128)(2,1)S(1)} %pad_maximum_fusion.1), channel_id=1, source_target_pairs={{0,3},{1,0},{2,1},{3,2},{4,7},{5,4},{6,5},{7,6},{8,11},{9,8},{10,9... | collective-permute-start | bytes 1843208 | tf_op jit(solution)/shard_map/ppermute | solution.py:34
  47.8 18.6 %collective-permute-start.5 = (bf16[480,640]{1,0:T(8,128)(2,1)S(1)}, bf16[480,640]{1,0:T(8,128)(2,1)S(1)}, u32[]{:S(2)}, u32[]{:S(2)}) collective-permute-start(bf16[480,640]{1,0:T(8,128)(2,1)S(1)} %pad_maximum_fusion), channel_id=1, source_target_pairs={{0,1},{1,2},{2,3},{3,0},{4,5},{5,6},{6,7},{7,4},{8,9},{9,10},{10,1... | collective-permute-start | bytes 1843208 | tf_op jit(solution)/shard_map/ppermute | solution.py:34
  52.5 10.3 %collective-permute-start.12 = (bf16[240,640]{1,0:T(8,128)(2,1)S(1)}, bf16[240,640]{1,0:T(8,128)(2,1)S(1)}, u32[]{:S(2)}, u32[]{:S(2)}) collective-permute-start(bf16[240,640]{1,0:T(8,128)(2,1)S(1)} %bitcast.69), channel_id=1, source_target_pairs={{0,4},{4,8},{8,12},{12,0},{1,5},{5,9},{9,13},{13,1},{2,6},{6,10},{... | collective-permute-start | bytes 921608 | tf_op jit(solution)/shard_map/ppermute | solution.py:34
  54.1 8.7 %collective-permute-start.13 = (bf16[240,640]{1,0:T(8,128)(2,1)S(1)}, bf16[240,640]{1,0:T(8,128)(2,1)S(1)}, u32[]{:S(2)}, u32[]{:S(2)}) collective-permute-start(bf16[240,640]{1,0:T(8,128)(2,1)S(1)} %bitcast.67), channel_id=1, source_target_pairs={{0,12},{4,0},{8,4},{12,8},{1,13},{5,1},{9,5},{13,9},{2,14},{6,2},{... | collective-permute-start | bytes 921608 | tf_op jit(solution)/shard_map/ppermute | solution.py:34
  63.0 19.7 %collective-permute-start.15 = (bf16[480,640]{1,0:T(8,128)(2,1)S(1)}, bf16[480,640]{1,0:T(8,128)(2,1)S(1)}, u32[]{:S(2)}, u32[]{:S(2)}) collective-permute-start(bf16[480,640]{1,0:T(8,128)(2,1)S(1)} %pad_maximum_fusion.3), channel_id=1, source_target_pairs={{0,12},{4,0},{8,4},{12,8},{1,13},{5,1},{9,5},{13,9},{2,14},{6,2},{... | collective-permute-start | bytes 1843208 | tf_op jit(solution)/shard_map/ppermute | solution.py:34
  66.3 20.1 %collective-permute-start.14 = (bf16[480,640]{1,0:T(8,128)(2,1)S(1)}, bf16[480,640]{1,0:T(8,128)(2,1)S(1)}, u32[]{:S(2)}, u32[]{:S(2)}) collective-permute-start(bf16[480,640]{1,0:T(8,128)(2,1)S(1)} %pad_maximum_fusion.2), channel_id=1, source_target_pairs={{0,4},{4,8},{8,12},{12,0},{1,5},{5,9},{9,13},{13,1},{2,6},{6,10},{... | collective-permute-start | bytes 1843208 | tf_op jit(solution)/shard_map/ppermute | solution.py:34
  66.8 22.8 %collective-permute-start.10 = (bf16[120,640]{1,0:T(8,128)(2,1)S(1)}, bf16[120,640]{1,0:T(8,128)(2,1)S(1)}, u32[]{:S(2)}, u32[]{:S(2)}) collective-permute-start(bf16[120,640]{1,0:T(8,128)(2,1)S(1)} %get-tuple-element.69), channel_id=1, source_target_pairs={{0,8},{4,12},{8,0},{12,4},{1,9},{5,13},{9,1},{13,5},{2,10},{6,14},... | collective-permute-start | bytes 460808 | tf_op jit(solution)/shard_map/ppermute | solution.py:34
  68.7 21.6 %collective-permute-start.9 = (bf16[120,640]{1,0:T(8,128)(2,1)S(1)}, bf16[120,640]{1,0:T(8,128)(2,1)S(1)}, u32[]{:S(2)}, u32[]{:S(2)}) collective-permute-start(bf16[120,640]{1,0:T(8,128)(2,1)S(1)} %get-tuple-element.70), channel_id=1, source_target_pairs={{0,12},{4,0},{8,4},{12,8},{1,13},{5,1},{9,5},{13,9},{2,14},{6,2},{... | collective-permute-start | bytes 460808 | tf_op jit(solution)/shard_map/ppermute | solution.py:34
  70.2 20.2 %collective-permute-start.8 = (bf16[120,640]{1,0:T(8,128)(2,1)S(1)}, bf16[120,640]{1,0:T(8,128)(2,1)S(1)}, u32[]{:S(2)}, u32[]{:S(2)}) collective-permute-start(bf16[120,640]{1,0:T(8,128)(2,1)S(1)} %get-tuple-element.68), channel_id=1, source_target_pairs={{0,4},{4,8},{8,12},{12,0},{1,5},{5,9},{9,13},{13,1},{2,6},{6,10},{... | collective-permute-start | bytes 460808 | tf_op jit(solution)/shard_map/ppermute | solution.py:34
  86.7 6.8 %collective-permute-start.18 = (bf16[120,640]{1,0:T(8,128)(2,1)S(1)}, bf16[120,640]{1,0:T(8,128)(2,1)S(1)}, u32[]{:S(2)}, u32[]{:S(2)}) collective-permute-start(bf16[120,640]{1,0:T(8,128)(2,1)S(1)} %get-tuple-element.78), channel_id=1, source_target_pairs={{0,2},{1,3},{2,0},{3,1},{4,6},{5,7},{6,4},{7,5},{8,10},{9,11},{10,... | collective-permute-start | bytes 460808 | tf_op jit(solution)/shard_map/ppermute | solution.py:34
  88.3 6.9 %collective-permute-start.17 = (bf16[120,640]{1,0:T(8,128)(2,1)S(1)}, bf16[120,640]{1,0:T(8,128)(2,1)S(1)}, u32[]{:S(2)}, u32[]{:S(2)}) collective-permute-start(bf16[120,640]{1,0:T(8,128)(2,1)S(1)} %get-tuple-element.79), channel_id=1, source_target_pairs={{0,3},{1,0},{2,1},{3,2},{4,7},{5,4},{6,5},{7,6},{8,11},{9,8},{10,9... | collective-permute-start | bytes 460808 | tf_op jit(solution)/shard_map/ppermute | solution.py:34
  89.6 6.4 %collective-permute-start.16 = (bf16[120,640]{1,0:T(8,128)(2,1)S(1)}, bf16[120,640]{1,0:T(8,128)(2,1)S(1)}, u32[]{:S(2)}, u32[]{:S(2)}) collective-permute-start(bf16[120,640]{1,0:T(8,128)(2,1)S(1)} %get-tuple-element.77), channel_id=1, source_target_pairs={{0,1},{1,2},{2,3},{3,0},{4,5},{5,6},{6,7},{7,4},{8,9},{9,10},{10,1... | collective-permute-start | bytes 460808 | tf_op jit(solution)/shard_map/ppermute | solution.py:34
  129.0 1.7 %collective-permute-start.19 = (bf16[6,40,640]{2,1,0:T(8,128)(2,1)S(1)}, bf16[6,40,640]{2,1,0:T(8,128)(2,1)S(1)}, u32[]{:S(2)}, u32[]{:S(2)}) collective-permute-start(bf16[6,40,640]{2,1,0:T(8,128)(2,1)S(1)} %reshape.172.mine), channel_id=1, source_target_pairs={{0,16},{16,0},{1,17},{17,1},{2,18},{18,2},{3,19},{19,3},{4,20},{20... | collective-permute-start | bytes 921608 | tf_op jit(solution)/shard_map/ppermute | solution.py:385
